TPU v7x, 128 devices: a whole 4x4x4 slice. The times are simulated.
128 devices in a mesh: dp: 16 (over z, y), mp: 8 (over x, core).
Axes of the slice: x: 4, y: 4, z: 4, core: 2. Of those that a mesh axis runs over, the one named last changes fastest.
Arguments:
- residual: bfloat16 [2048, 4096], P('dp', 'mp'), may hold values from -18 to 18
- queries: bfloat16 [2048, 4096], P('dp', 'mp'), may hold values from -20 to 20
- new_keys: bfloat16 [2048, 1024], P('dp', 'mp'), may hold values from -6 to 6
- new_values: bfloat16 [2048, 1024], P('dp', 'mp'), may hold values from -6 to 6
- cache_keys: bfloat16 [2048, 16, 1024], P('dp', None, 'mp'), may hold values from -6 to 6
- cache_values: bfloat16 [2048, 16, 1024], P('dp', None, 'mp'), may hold values from -6 to 6
- cache_len: int32 [1024], replicated, may hold values from 1 to 128, 16384 in all
- page_order: int32 [2048], replicated, may hold values from 0 to 2047, each once
- out_proj: bfloat16 [4096, 4096], P('mp'), may hold values from -0.09375 to 0.09375
- attn_gain: float32 [4096], replicated, may hold values from 0.25 to 1.75
- routes: int32 [2048, 2], P('dp'), may hold values from 0 to 7, all different within a row; in each aligned block of 128 rows (0 to 127, 128 to 255, ...) at most 48 rows name the same one
- route_weight: float32 [2048, 2], P('dp'), may hold values from 0.1 to 1
- gate_proj: bfloat16 [4096, 98304], P(None, ('dp', 'mp')), may hold values from -0.09375 to 0.09375
- up_proj: bfloat16 [4096, 98304], P(None, ('dp', 'mp')), may hold values from -0.09375 to 0.09375
- down_proj: bfloat16 [98304, 4096], P(('dp', 'mp')), may hold values from -0.0546875 to 0.0546875
- final_gain: float32 [4096], P('mp'), may hold values from 0.25 to 1.75
Outputs:
- layer_out: bfloat16 [2048, 4096], P('dp', 'mp')
Inputs may be any that keep to these rules, and one draw needn't show every extreme that they name: `routes`: in each aligned block of 128 rows (the rows of one dp group) no expert is named by more than 48 rows, a bound that some block reaches; a row's two experts differ. `cache_len`: the lengths sum to 16384, and the longest is exactly 128. `page_order`: each page number appears once; pages past the last request's are unused.
All inputs are finite; a program needn't handle non-finite values.
Results may differ from a plain program's by a relative error of at most 0.008.
Values may be sent and summed in bfloat16 or wider, within the bound.
A program may use at most 128 MiB of HBM per device.

v0:
```python
import jax
import jax.numpy as jnp
from jax import lax
from jax.sharding import PartitionSpec as P

D = 4096
HQ = 32
KVH = 8
HD = 128
E = 8
PAGE = 16
DEC = 64
PRE = 64
C = 48
neg_big = -1e30
eps_norm = 1e-05


def page_owner(page_ids, page_order, cache_len):
    page_count = (cache_len + PAGE - 1) // PAGE
    page_ends = jnp.cumsum(page_count)
    page_first = page_ends - page_count
    pool_iota = lax.broadcasted_iota(jnp.int32, (1, page_order.shape[0]), 1)
    order_pos = jnp.sum(jnp.where(page_order[None, :] == page_ids[:, None], pool_iota, 0), axis=1)
    owners = jnp.sum((page_ends[None, :] <= order_pos[:, None]).astype(jnp.int32), axis=1)
    request_iota = lax.broadcasted_iota(jnp.int32, (1, cache_len.shape[0]), 1)
    chosen = request_iota == owners[:, None]
    first_own = jnp.sum(jnp.where(chosen, page_first[None, :], 0), axis=1)
    length_own = jnp.sum(jnp.where(chosen, cache_len[None, :], 0), axis=1)
    offsets = lax.broadcasted_iota(jnp.int32, (1, PAGE), 1)
    key_pos = (order_pos - first_own)[:, None] * PAGE + offsets
    return (owners, key_pos < length_own[:, None])


def page_partials(page_queries, key_pages, value_pages, key_ok, scale):
    scores = (
        jnp.einsum("pkgh,pokh->pkgo", page_queries, key_pages, preferred_element_type=jnp.float32)
        * scale
    )
    wide_mask = key_ok[:, None, None, :]
    masked = jnp.where(wide_mask, scores, neg_big)
    maxima = jnp.max(masked, axis=3)
    weights = jnp.where(wide_mask, jnp.exp(masked - maxima[..., None]), 0.0)
    totals = jnp.sum(weights, axis=3)
    weighted = jnp.einsum(
        "pkgo,pokh->pkgh",
        weights,
        value_pages.astype(jnp.float32),
        precision=lax.Precision.HIGHEST,
        preferred_element_type=jnp.float32,
    )
    return (maxima, totals, weighted)


def fold_pages(maxima, totals, weighted, owned, local_owner):
    top_score = jnp.max(jnp.where(owned[:, :, None, None], maxima[:, None], neg_big), axis=0)
    page_top = top_score[local_owner]
    factors = jnp.exp(maxima - page_top)
    owned_float = owned.astype(jnp.float32)
    sums = jnp.einsum("pr,pkg->rkg", owned_float, totals * factors, precision=lax.Precision.HIGHEST)
    values = jnp.einsum(
        "pr,pkgh->rkgh", owned_float, weighted * factors[..., None], precision=lax.Precision.HIGHEST
    )
    return (top_score, sums, values)


def local(
    residual,
    queries,
    new_keys,
    new_values,
    cache_keys,
    cache_values,
    cache_len,
    page_order,
    out_proj,
    attn_gain,
    routes,
    route_weight,
    gate_proj,
    up_proj,
    down_proj,
    final_gain,
):
    dp_count = lax.axis_size("dp")
    dp_index = lax.axis_index("dp")
    mp_index = lax.axis_index("mp")
    scale = HD ** (-0.5)
    kv_local = new_keys.shape[1] // HD
    group_size = HQ // KVH
    width_local = residual.shape[1]
    pool_local = cache_keys.shape[0]
    request_total = cache_len.shape[0]
    query_heads = queries[:DEC].reshape(DEC, kv_local, group_size, HD)
    gathered = lax.all_gather(queries[:DEC], "dp", axis=0, tiled=True)
    gathered_heads = gathered.reshape(request_total, kv_local, group_size, HD)
    page_ids = dp_index * pool_local + lax.broadcasted_iota(jnp.int32, (pool_local,), 0)
    owners, key_ok = page_owner(page_ids, page_order, cache_len)
    live = owners < request_total
    local_owner = jnp.minimum(owners, request_total - 1)
    key_ok = key_ok & live[:, None]
    key_pages = cache_keys.reshape(pool_local, PAGE, kv_local, HD)
    value_pages = cache_values.reshape(pool_local, PAGE, kv_local, HD)
    page_queries = gathered_heads[local_owner]
    maxima, totals, weighted = page_partials(page_queries, key_pages, value_pages, key_ok, scale)
    owned = (local_owner[:, None] == lax.broadcasted_iota(jnp.int32, (1, request_total), 1)) & live[
        :, None
    ]
    maxima, totals, weighted = fold_pages(maxima, totals, weighted, owned, local_owner)
    maxima = maxima.reshape(dp_count, DEC, kv_local, group_size)
    totals = totals.reshape(dp_count, DEC, kv_local, group_size)
    weighted = weighted.reshape(dp_count, DEC, kv_local, group_size, HD)
    maxima, totals, weighted = (
        lax.all_to_all(maxima, "dp", split_axis=0, concat_axis=0, tiled=True),
        lax.all_to_all(totals, "dp", split_axis=0, concat_axis=0, tiled=True),
        lax.all_to_all(weighted, "dp", split_axis=0, concat_axis=0, tiled=True),
    )
    top_cache = jnp.max(maxima, axis=0)
    factors = jnp.exp(maxima - top_cache[None])
    cache_state = (
        top_cache,
        jnp.sum(totals * factors, axis=0),
        jnp.sum(weighted * factors[..., None], axis=0),
    )
    self_keys = new_keys[:DEC].reshape(DEC, kv_local, HD)
    self_values = new_values[:DEC].reshape(DEC, kv_local, HD).astype(jnp.float32)
    self_score = (
        jnp.einsum("rkgh,rkh->rkg", query_heads, self_keys, preferred_element_type=jnp.float32)
        * scale
    )
    cache_top, cache_total, cache_sum = cache_state
    top_score = jnp.maximum(cache_top, self_score)
    cache_factor = jnp.exp(cache_top - top_score)
    self_factor = jnp.exp(self_score - top_score)
    numerator = (
        cache_sum * cache_factor[..., None] + self_factor[..., None] * self_values[:, :, None, :]
    )
    denominator = cache_total * cache_factor + self_factor
    decode_out = (numerator / denominator[..., None]).astype(jnp.bfloat16).reshape(DEC, -1)
    prompt_q = queries[DEC:].reshape(PRE, kv_local, group_size, HD)
    prompt_k = new_keys[DEC:].reshape(PRE, kv_local, HD)
    prompt_v = new_values[DEC:].reshape(PRE, kv_local, HD).astype(jnp.float32)
    prompt_scores = (
        jnp.einsum("qkgh,tkh->kgqt", prompt_q, prompt_k, preferred_element_type=jnp.float32) * scale
    )
    causal = lax.broadcasted_iota(jnp.int32, (PRE, PRE), 0) >= lax.broadcasted_iota(
        jnp.int32, (PRE, PRE), 1
    )
    masked = jnp.where(causal, prompt_scores, neg_big)
    top_prompt = jnp.max(masked, axis=-1, keepdims=True)
    prompt_weights = jnp.where(causal, jnp.exp(masked - top_prompt), 0.0)
    prompt_num = jnp.einsum(
        "kgqt,tkh->qkgh",
        prompt_weights,
        prompt_v,
        precision=lax.Precision.HIGHEST,
        preferred_element_type=jnp.float32,
    )
    prompt_den = jnp.sum(prompt_weights, axis=-1).transpose(2, 0, 1)
    prompt_out = (prompt_num / prompt_den[..., None]).astype(jnp.bfloat16).reshape(PRE, -1)
    attn = jnp.concatenate([decode_out, prompt_out], axis=0)
    head_terms = jnp.dot(attn, out_proj, preferred_element_type=jnp.float32)
    column_start = mp_index * width_local
    own_columns = lax.dynamic_slice_in_dim(
        head_terms, column_start, width_local, 1
    ) + residual.astype(jnp.float32)
    head_terms = lax.dynamic_update_slice_in_dim(head_terms, own_columns, column_start, 1)
    hidden_full = lax.psum(head_terms, "mp")
    normed = (
        hidden_full
        * lax.rsqrt(jnp.mean(hidden_full * hidden_full, axis=1, keepdims=True) + eps_norm)
        * attn_gain[None, :]
    ).astype(jnp.bfloat16)
    hidden_cols = lax.dynamic_slice_in_dim(hidden_full, column_start, width_local, 1)
    tok_rows = residual.shape[0]
    pairs = routes.reshape(-1)
    onehot = (pairs[:, None] == lax.broadcasted_iota(jnp.int32, (1, E), 1)).astype(jnp.int32)
    slots = jnp.sum((jnp.cumsum(onehot, axis=0) - onehot) * onehot, axis=1)
    target = pairs * C + slots
    cells = lax.broadcasted_iota(jnp.int32, (1, E * C), 1)
    hits = (target[:, None] == cells).reshape(tok_rows, 2, E * C)
    dispatch = jnp.any(hits, axis=1).astype(jnp.bfloat16)
    combine = jnp.sum(jnp.where(hits, route_weight[:, :, None], 0.0), axis=1)
    buffer = lax.dot_general(
        dispatch, normed, (((0,), (0,)), ((), ())), preferred_element_type=jnp.float32
    ).astype(jnp.bfloat16)
    send = jnp.repeat(buffer.reshape(E, C, normed.shape[1]), dp_count // E, axis=0)
    arrived = lax.all_to_all(send, "dp", split_axis=0, concat_axis=0, tiled=True)
    gate_sum = jnp.einsum("scd,df->scf", arrived, gate_proj, preferred_element_type=jnp.float32)
    up_sum = jnp.einsum("scd,df->scf", arrived, up_proj, preferred_element_type=jnp.float32)
    hidden = (jax.nn.silu(gate_sum) * up_sum).astype(jnp.bfloat16)
    down_part = jnp.einsum("scf,fd->scd", hidden, down_proj, preferred_element_type=jnp.float32)
    shares = lax.psum_scatter(
        down_part.astype(jnp.bfloat16), "mp", scatter_dimension=2, tiled=True
    ).astype(jnp.float32)
    returned = lax.all_to_all(shares, "dp", split_axis=0, concat_axis=0, tiled=True)
    back = (
        returned.reshape(E, dp_count // E, C, width_local).sum(axis=1).reshape(E * C, width_local)
    )
    moe_rows = jnp.dot(
        combine, back, precision=lax.Precision.HIGHEST, preferred_element_type=jnp.float32
    )
    mixed = hidden_cols + moe_rows
    square_last = lax.psum(jnp.sum(mixed * mixed, axis=1), "mp")
    scaled = mixed * lax.rsqrt(square_last / D + eps_norm)[:, None] * final_gain[None, :]
    return scaled.astype(jnp.bfloat16)


def solution(mesh):
    return jax.shard_map(
        local,
        mesh=mesh,
        in_specs=(
            P("dp", "mp"),
            P("dp", "mp"),
            P("dp", "mp"),
            P("dp", "mp"),
            P("dp", None, "mp"),
            P("dp", None, "mp"),
            P(),
            P(),
            P("mp", None),
            P(),
            P("dp", None),
            P("dp", None),
            P(None, ("dp", "mp")),
            P(None, ("dp", "mp")),
            P(("dp", "mp"), None),
            P("mp"),
        ),
        out_specs=P("dp", "mp"),
        check_vma=False,
    )
```

profile of v0, /device:TPU:0, one launch (start us, length us, event | category | flops | bytes accessed | tf_op | source)
XLA Modules:
  0.0 386.7 jit_solution(8558500685093032469)
XLA Ops:
  6.5 1.6 fusion.67
  8.2 0.7 fusion.64
  8.9 0.3 reduce-window.15
  9.4 0.8 fusion.63
  10.1 1.0 select_reduce_fusion.1
  11.3 0.9 select_reduce_fusion.3
  12.6 42.3 %all-gather.2.cloned.1.call-done = bf16[1024,512]{1,0:T(8,128)(2,1)} async-done(((bf16[64,512]{1,0:T(8,128)(2,1)}), bf16[1024,512]{1,0:T(8,128)(2,1)}) %all-gather.2.cloned.1.call-update) | async-done | bytes 1048592 | tf_op jit(solution)/shard_map/all_gather | solution.py:95
  54.9 1.3 reshape.430
  56.2 0.7 gather_fusion
  57.0 0.5 fusion.69
  57.5 0.3 select_reduce_fusion
  58.1 0.7 gather_fusion.1
  58.7 0.4 fusion.25
  59.1 0.8 fusion.70
  59.9 0.7 reshape.468
  60.6 4.9 %all-to-all-start.2 = ((f32[16,1,256]{2,1,0:T(1,128)}), f32[16,1,256]{2,1,0:T(1,128)S(1)}, u32[]{:S(2)}, u32[]{:S(2)}) async-start(f32[16,1,256]{2,1,0:T(1,128)} %reshape.468), calls=%async_computation.2 | async-start | bytes 32768 | tf_op jit(solution)/shard_map/all_to_all | solution.py:115
  65.6 0.7 fusion.7
  66.5 0.7 reshape.466
  67.2 5.9 %all-to-all-done.2 = f32[16,1,256]{2,1,0:T(1,128)S(1)} async-done(((f32[16,1,256]{2,1,0:T(1,128)}), f32[16,1,256]{2,1,0:T(1,128)S(1)}, u32[]{:S(2)}, u32[]{:S(2)}) %all-to-all-start.2) | async-done | bytes 16416 | tf_op jit(solution)/shard_map/all_to_all | solution.py:115
  73.1 3.5 all-to-all-start.1
  76.6 2.4 convolution_bitcast_fusion
  79.0 5.1 %all-to-all-done.1 = f32[16,1,256]{2,1,0:T(1,128)S(1)} async-done(((f32[16,1,256]{2,1,0:T(1,128)}), f32[16,1,256]{2,1,0:T(1,128)S(1)}, u32[]{:S(2)}, u32[]{:S(2)}) %all-to-all-start.1) | async-done | bytes 16416 | tf_op jit(solution)/shard_map/all_to_all | solution.py:114
  84.2 3.7 all-to-all-start
  88.6 0.3 fusion.12
  89.0 0.5 broadcast.295
  89.5 0.7 reduce.15
  90.3 0.7 reduce.14
  91.1 24.1 %all-to-all-done = f32[16,64,1,4,128]{4,1,3,2,0:T(8,128)S(1)} async-done(((f32[16,64,1,4,128]{4,1,3,2,0:T(8,128)}), f32[16,64,1,4,128]{4,1,3,2,0:T(8,128)S(1)}, u32[]{:S(2)}, u32[]{:S(2)}) %all-to-all-start) | async-done | bytes 2097184 | tf_op jit(solution)/shard_map/all_to_all | solution.py:116
  115.2 0.7 bitcast_reduce_fusion
  116.1 2.9 fusion.26
  119.1 1.3 copy-done.2
  120.9 0.6 reduce-window.19
  122.2 60.5 %all-reduce.2.cloned.1.call-done = f32[128,4096]{1,0:T(8,128)} async-done(((f32[128,4096]{1,0:T(8,128)}), f32[128,4096]{1,0:T(8,128)}) %all-reduce.2.cloned.1.call-update) | async-done | bytes 2097168 | tf_op jit(solution)/shard_map/psum | solution.py:168
  182.7 2.0 multiply_reduce_fusion
  185.0 1.1 convolution_convert_fusion.1
  186.0 0.8 broadcast_in_dim.146
  186.8 79.0 %all_to_all.25 = bf16[16,48,4096]{2,1,0:T(8,128)(2,1)S(1)} all-to-all(bf16[16,48,4096]{2,1,0:T(8,128)(2,1)S(1)} %bitcast.149), channel_id=1, replica_groups=mesh['dp'=16,'mp'=8] {'dp'}, dimensions={0} | all-to-all | bytes 12582912 | tf_op jit(solution)/shard_map/all_to_all | solution.py:188
  265.8 7.5 %fusion.1 = f32[16,48,768]{2,1,0:T(8,128)S(1)} fusion(bf16[16,48,4096]{2,1,0:T(8,128)(2,1)S(1)} %all_to_all.25, bf16[4096,768]{1,0:T(8,128)(2,1)} %param.29), kind=kOutput, calls=%fused_computation.4 | convolution fusion | flops 4831838208 | bytes 14942208 | tf_op jit(solution)/shard_map/scd,df->scf/dot_general | solution.py:190
  273.3 5.3 %multiply_convert_fusion = bf16[16,48,768]{2,1,0:T(8,128)(2,1)S(1)} fusion(f32[16,48,768]{2,1,0:T(8,128)S(1)} %fusion.1, bf16[16,48,4096]{2,1,0:T(8,128)(2,1)S(1)} %all_to_all.25, bf16[4096,768]{1,0:T(8,128)(2,1)S(1)} %bitcast.157), kind=kOutput, calls=%fused_computation.9 | convolution fusion | flops 4835377152 | bytes 16121856 | tf_op jit(solution)/shard_map/scd,df->scf/dot_general | solution.py:189
  278.7 6.9 %convolution_convert_fusion = bf16[16,48,4096]{2,1,0:T(8,128)(2,1)} fusion(bf16[16,48,768]{2,1,0:T(8,128)(2,1)S(1)} %multiply_convert_fusion, bf16[768,4096]{1,0:T(8,128)(2,1)S(1)} %bitcast.159), kind=kOutput, calls=%fused_computation.2 | convolution fusion | flops 4834983936 | bytes 13762560 | tf_op jit(solution)/shard_map/scf,fd->scd/dot_general | solution.py:192
  285.6 41.4 %reduce-scatter.2.cloned.1.call-done = bf16[16,48,512]{2,1,0:T(8,128)(2,1)} async-done(((bf16[16,48,4096]{2,1,0:T(8,128)(2,1)}), bf16[16,48,512]{2,1,0:T(8,128)(2,1)}) %reduce-scatter.2.cloned.1.call-update) | async-done | bytes 786448 | tf_op jit(solution)/shard_map/reduce_scatter | solution.py:193
  327.0 2.5 convert_element_type.63
  329.5 7.0 %all-to-all-start.4 = ((f32[16,48,512]{2,1,0:T(8,128)}), f32[16,48,512]{2,1,0:T(8,128)}, u32[]{:S(2)}, u32[]{:S(2)}) async-start(f32[16,48,512]{2,1,0:T(8,128)} %convert_element_type.63), calls=%async_computation.5 | async-start | bytes 3145728 | tf_op jit(solution)/shard_map/all_to_all | solution.py:196
  336.7 23.3 %all-to-all-done.4 = f32[16,48,512]{2,1,0:T(8,128)} async-done(((f32[16,48,512]{2,1,0:T(8,128)}), f32[16,48,512]{2,1,0:T(8,128)}, u32[]{:S(2)}, u32[]{:S(2)}) %all-to-all-start.4) | async-done | bytes 1572896 | tf_op jit(solution)/shard_map/all_to_all | solution.py:196
  360.1 1.6 bitcast_reduce_fusion.1
  361.7 0.7 multiply_reduce_fusion.1
  362.4 17.0 %psum.15 = f32[128]{0:T(128)S(1)} all-reduce(f32[128]{0:T(128)S(1)} %get-tuple-element.20), channel_id=1, replica_groups=mesh['dp'=16,'mp'=8] {'mp'}, use_global_device_ids=true, to_apply=%region_24.25 | all-reduce | flops 128 | bytes 1024 | tf_op jit(solution)/shard_map/psum | solution.py:204
  379.4 0.8 multiply_convert_fusion.3
  (93 shorter events, 4.1 us)
Async XLA Ops:
  6.5 59.0 %copy-start = (bf16[128,16,128]{2,1,0:T(8,128)(2,1)S(1)}, bf16[128,16,128]{2,1,0:T(8,128)(2,1)}, u32[]{:S(2)}) copy-start(bf16[128,16,128]{2,1,0:T(8,128)(2,1)} %param.21) | copy-start | bytes 1572868
  6.5 50.5 %copy-start.5 = (bf16[128,16,128]{2,1,0:T(8,128)(2,1)S(1)}, bf16[128,16,128]{2,1,0:T(8,128)(2,1)}, u32[]{:S(2)}) copy-start(bf16[128,16,128]{2,1,0:T(8,128)(2,1)} %param.20) | copy-start | bytes 1572868
  6.5 48.4 %all-gather.2.cloned.1.call-start = ((), (), s32[]{:S(2)}) async-start(), calls=%async_computation.6 | async-start | bytes 1114112 | tf_op jit(solution)/shard_map/all_gather | solution.py:95
  60.6 12.5 %all-to-all-start.2 = ((f32[16,1,256]{2,1,0:T(1,128)}), f32[16,1,256]{2,1,0:T(1,128)S(1)}, u32[]{:S(2)}, u32[]{:S(2)}) async-start(f32[16,1,256]{2,1,0:T(1,128)} %reshape.468), calls=%async_computation.2 | async-start | bytes 32768 | tf_op jit(solution)/shard_map/all_to_all | solution.py:115
  73.1 11.0 %all-to-all-start.1 = ((f32[16,1,256]{2,1,0:T(1,128)}), f32[16,1,256]{2,1,0:T(1,128)S(1)}, u32[]{:S(2)}, u32[]{:S(2)}) async-start(f32[16,1,256]{2,1,0:T(1,128)} %reshape.466), calls=%async_computation.1 | async-start | bytes 32768 | tf_op jit(solution)/shard_map/all_to_all | solution.py:114
  79.0 8.9 %copy-start.4 = (bf16[64,512]{1,0:T(8,128)(2,1)S(1)}, bf16[64,512]{1,0:T(8,128)(2,1)}, u32[]{:S(2)}) copy-start(bf16[64,512]{1,0:T(8,128)(2,1)} %get-tuple-element.12) | copy-start | bytes 196612
  79.0 9.0 %copy-start.7 = (bf16[128,128]{1,0:T(8,128)(2,1)S(1)}, bf16[128,128]{1,0:T(8,128)(2,1)}, u32[]{:S(2)}) copy-start(bf16[128,128]{1,0:T(8,128)(2,1)} %param.18) | copy-start | bytes 98308
  79.0 9.5 %copy-start.9 = (bf16[128,128]{1,0:T(8,128)(2,1)S(1)}, bf16[128,128]{1,0:T(8,128)(2,1)}, u32[]{:S(2)}) copy-start(bf16[128,128]{1,0:T(8,128)(2,1)} %param.19) | copy-start | bytes 98308
  84.2 31.0 %all-to-all-start = ((f32[16,64,1,4,128]{4,1,3,2,0:T(8,128)}), f32[16,64,1,4,128]{4,1,3,2,0:T(8,128)S(1)}, u32[]{:S(2)}, u32[]{:S(2)}) async-start(f32[16,64,1,4,128]{4,1,3,2,0:T(8,128)} %convolution_bitcast_fusion), calls=%async_computation | async-start | bytes 4194304 | tf_op jit(solution)/shard_map/all_to_all | solution.py:116
  87.9 94.8 %all-reduce.2.cloned.1.call-start = ((), (), s32[]{:S(2)}) async-start(), calls=%async_computation.7 | async-start | bytes 4194304 | tf_op jit(solution)/shard_map/psum | solution.py:168
  116.1 3.0 copy-start.6
  119.0 1.4 copy-start.10
  119.1 1.3 copy-start.2
  119.1 65.6 %copy-start.8 = (f32[4096]{0:T(1024)S(1)}, f32[4096]{0:T(1024)}, u32[]{:S(2)}) copy-start(f32[4096]{0:T(1024)} %param.25) | copy-start | bytes 49156
  120.4 206.6 %reduce-scatter.2.cloned.1.call-start = ((), (), s32[]{:S(2)}) async-start(), calls=%async_computation.8 | async-start | bytes 7077888 | tf_op jit(solution)/shard_map/reduce_scatter | solution.py:193
  182.7 2.2 copy-start.3
  186.8 86.5 %slice-start = ((s8[6291456]{0:T(1024)(128)(4,1)}), s8[4194304]{0:T(1024)(128)(4,1)S(1)}, s32[]{:S(2)}) async-start(s8[6291456]{0:T(1024)(128)(4,1)} %bitcast.156), calls=%async_computation.9 | async-start | bytes 8388608
  265.8 7.5 %slice-start.1 = ((s8[6291456]{0:T(1024)(128)(4,1)}), s8[2097152]{0:T(1024)(128)(4,1)S(1)}, s32[]{:S(2)}) async-start(s8[6291456]{0:T(1024)(128)(4,1)} %bitcast.156), calls=%async_computation.10 | async-start | bytes 4194304
  265.8 12.8 %slice-start.2 = ((s8[6291456]{0:T(1024)(128)(4,1)}), s8[4194304]{0:T(1024)(128)(4,1)S(1)}, s32[]{:S(2)}) async-start(s8[6291456]{0:T(1024)(128)(4,1)} %bitcast.158), calls=%async_computation.11 | async-start | bytes 8388608
  273.3 5.3 %slice-start.3 = ((s8[6291456]{0:T(1024)(128)(4,1)}), s8[2097152]{0:T(1024)(128)(4,1)S(1)}, s32[]{:S(2)}) async-start(s8[6291456]{0:T(1024)(128)(4,1)} %bitcast.158), calls=%async_computation.12 | async-start | bytes 4194304
  285.6 51.0 %copy-start.12 = (f32[128,2]{0,1:T(2,128)S(1)}, f32[128,2]{0,1:T(2,128)}, u32[]{:S(2)}) copy-start(f32[128,2]{0,1:T(2,128)} %param.27) | copy-start | bytes 3076
  329.5 30.5 %all-to-all-start.4 = ((f32[16,48,512]{2,1,0:T(8,128)}), f32[16,48,512]{2,1,0:T(8,128)}, u32[]{:S(2)}, u32[]{:S(2)}) async-start(f32[16,48,512]{2,1,0:T(8,128)} %convert_element_type.63), calls=%async_computation.5 | async-start | bytes 3145728 | tf_op jit(solution)/shard_map/all_to_all | solution.py:196
  336.6 42.8 %copy-start.11 = (f32[512]{0:T(512)S(1)}, f32[512]{0:T(512)}, u32[]{:S(2)}) copy-start(f32[512]{0:T(512)} %param.31) | copy-start | bytes 6148
  336.6 43.6 %copy-start.1 = (bf16[128,16,128]{2,1,0:T(8,128)(2,1)S(1)}, bf16[128,16,128]{2,1,0:T(8,128)(2,1)}, u32[]{:S(2)}) copy-start(bf16[128,16,128]{2,1,0:T(8,128)(2,1)} %param.21) | copy-start | bytes 1572868
Sparse Core Ops, SparseCore 0:
  9.5 45.3 all-gather.1
  120.5 62.1 all-reduce.1
  285.7 41.2 reduce-scatter.1
where the time goes:
time: 387 us
  waiting for transfers between devices  203 us (52%)
  blocking collectives  96 us (25%)
  matrix products  29.4 us (8%)
  starting transfers between devices  19.3 us (5%)
  other arithmetic  15.1 us (4%)
  between operations  13.6 us (4%)
  local copies, waits for them, and re-layouts  10.6 us (3%)
    all_to_all x1, blocking collectives, local(): lax.all_to_all(send, 'dp', split_axis=0, concat_axis=0, tiled=True)  79 us
    psum x1, waiting for transfers between devices, local(): hidden_full = lax.psum(head_terms, 'mp')  60.5 us
    all_gather x1, waiting for transfers between devices, local(): gathered = lax.all_gather(queries[:DEC], 'dp', axis=0, tiled=True)  42.3 us
    reduce_scatter x1, waiting for transfers between devices, local(): lax.psum_scatter(down_part.astype(jnp.bfloat16), 'mp', scatter_dimension=...  41.4 us
    all_to_all x1, waiting for transfers between devices, local(): lax.all_to_all(weighted, 'dp', split_axis=0, concat_axis=0, tiled=True)  24.1 us
    all_to_all x1, waiting for transfers between devices, local(): lax.all_to_all(shares, 'dp', split_axis=0, concat_axis=0, tiled=True)  23.3 us
    psum x1, blocking collectives, local(): square_last = lax.psum(jnp.sum(mixed * mixed, axis=1), 'mp')  17 us
  transfers between devices with their start and end apart: 7, of which 7 were waited for; matrix products, arithmetic and copies ran while one was open for 3% of the time, Pallas kernels for 0%

commit v1 on v0

--- a/solution.py
+++ b/solution.py
@@ -92,7 +92,9 @@
     pool_local = cache_keys.shape[0]
     request_total = cache_len.shape[0]
     query_heads = queries[:DEC].reshape(DEC, kv_local, group_size, HD)
-    gathered = lax.all_gather(queries[:DEC], "dp", axis=0, tiled=True)
+    gathered = jnp.concatenate(
+        lax.all_to_all(jnp.stack([queries[:DEC]] * lax.axis_size("dp")), "dp", 0, 0), axis=0
+    )
     gathered_heads = gathered.reshape(request_total, kv_local, group_size, HD)
     page_ids = dp_index * pool_local + lax.broadcasted_iota(jnp.int32, (pool_local,), 0)
     owners, key_ok = page_owner(page_ids, page_order, cache_len)

time: 387 us -> 365 us (0.943)
  waiting for transfers between devices: 203 us -> 177 us
  starting transfers between devices: 19.3 us -> 26.1 us
    all_gather x1 -> x0, waiting for transfers between devices: 42.3 us -> none  [local(): gathered = lax.all_gather(queries[:DEC], 'dp', axis=0, tiled=True)]
    all_to_all x0 -> x1, waiting for transfers between devices: none -> 15.9 us  [local(): lax.all_to_all(jnp.stack([queries[:DEC]] * lax.axis_size('dp')), 'dp', 0, 0)]
    all_to_all x0 -> x1, starting transfers between devices: none -> 8.26 us  [local(): lax.all_to_all(jnp.stack([queries[:DEC]] * lax.axis_size('dp')), 'dp', 0, 0)]
where the time goes in v1:
time: 365 us; the launch traced here: 364 us
  waiting for transfers between devices  177 us (48%)
  blocking collectives  96 us (26%)
  matrix products  29.4 us (8%)
  starting transfers between devices  26.1 us (7%)
  between operations  14 us (4%)
  other arithmetic  12.3 us (3%)
  local copies, waits for them, and re-layouts  9.97 us (3%)
    all_to_all x1, blocking collectives, local(): lax.all_to_all(send, 'dp', split_axis=0, concat_axis=0, tiled=True)  79 us
    psum x1, waiting for transfers between devices, local(): hidden_full = lax.psum(head_terms, 'mp')  60.5 us
    reduce_scatter x1, waiting for transfers between devices, local(): lax.psum_scatter(down_part.astype(jnp.bfloat16), 'mp', scatter_dimension=...  41.5 us
    all_to_all x1, waiting for transfers between devices, local(): lax.all_to_all(weighted, 'dp', split_axis=0, concat_axis=0, tiled=True)  24.2 us
    all_to_all x1, waiting for transfers between devices, local(): lax.all_to_all(shares, 'dp', split_axis=0, concat_axis=0, tiled=True)  23.3 us
    psum x1, blocking collectives, local(): square_last = lax.psum(jnp.sum(mixed * mixed, axis=1), 'mp')  17 us
    all_to_all x1, waiting for transfers between devices, local(): lax.all_to_all(jnp.stack([queries[:DEC]] * lax.axis_size('dp')), 'dp', 0, 0)  15.9 us
    all_to_all x1, starting transfers between devices, local(): lax.all_to_all(jnp.stack([queries[:DEC]] * lax.axis_size('dp')), 'dp', 0, 0)  8.26 us
  transfers between devices with their start and end apart: 7, of which 7 were waited for; matrix products, arithmetic and copies ran while one was open for 3% of the time, Pallas kernels for 0%

profile of v1, /device:TPU:0, one launch (start us, length us, event | category | flops | bytes accessed | tf_op | source)
XLA Modules:
  0.0 364.3 jit_solution(3078497446411939452)
XLA Ops:
  6.5 0.9 fusion.67
  7.5 1.1 stack.2
  8.6 8.3 %all-to-all-start = ((bf16[16,64,512]{2,1,0:T(8,128)(2,1)}), bf16[16,64,512]{2,1,0:T(8,128)(2,1)S(1)}, u32[]{:S(2)}, u32[]{:S(2)}) async-start(bf16[16,64,512]{2,1,0:T(8,128)(2,1)} %stack.2), calls=%async_computation | async-start | bytes 2097152 | tf_op jit(solution)/shard_map/all_to_all | solution.py:96
  16.9 0.3 reduce-window.15
  17.5 0.3 select_reduce_fusion.1
  18.0 0.2 select_reduce_fusion.3
  18.6 15.9 %all-to-all-done = bf16[16,64,512]{2,1,0:T(8,128)(2,1)S(1)} async-done(((bf16[16,64,512]{2,1,0:T(8,128)(2,1)}), bf16[16,64,512]{2,1,0:T(8,128)(2,1)S(1)}, u32[]{:S(2)}, u32[]{:S(2)}) %all-to-all-start) | async-done | bytes 1048608 | tf_op jit(solution)/shard_map/all_to_all | solution.py:96
  34.5 0.3 reshape.428
  34.8 0.7 gather_fusion
  35.5 0.5 fusion.69
  36.1 0.3 select_reduce_fusion
  36.6 0.7 gather_fusion.1
  37.3 0.4 fusion.25
  37.6 0.8 fusion.70
  38.4 0.7 reshape.466
  39.1 3.5 all-to-all-start.3
  42.7 0.7 fusion.7
  43.6 0.7 reshape.464
  44.3 5.8 %all-to-all-done.3 = f32[16,1,256]{2,1,0:T(1,128)S(1)} async-done(((f32[16,1,256]{2,1,0:T(1,128)}), f32[16,1,256]{2,1,0:T(1,128)S(1)}, u32[]{:S(2)}, u32[]{:S(2)}) %all-to-all-start.3) | async-done | bytes 16416 | tf_op jit(solution)/shard_map/all_to_all | solution.py:117
  50.2 3.5 all-to-all-start.2
  53.7 2.4 convolution_bitcast_fusion
  56.1 5.1 %all-to-all-done.2 = f32[16,1,256]{2,1,0:T(1,128)S(1)} async-done(((f32[16,1,256]{2,1,0:T(1,128)}), f32[16,1,256]{2,1,0:T(1,128)S(1)}, u32[]{:S(2)}, u32[]{:S(2)}) %all-to-all-start.2) | async-done | bytes 16416 | tf_op jit(solution)/shard_map/all_to_all | solution.py:116
  61.2 3.7 %all-to-all-start.1 = ((f32[16,64,1,4,128]{4,1,3,2,0:T(8,128)}), f32[16,64,1,4,128]{4,1,3,2,0:T(8,128)S(1)}, u32[]{:S(2)}, u32[]{:S(2)}) async-start(f32[16,64,1,4,128]{4,1,3,2,0:T(8,128)} %convolution_bitcast_fusion), calls=%async_computation.1 | async-start | bytes 4194304 | tf_op jit(solution)/shard_map/all_to_all | solution.py:118
  65.6 0.3 fusion.12
  66.0 0.5 broadcast.297
  66.5 0.7 reduce.15
  67.3 0.7 reduce.14
  68.2 24.2 %all-to-all-done.1 = f32[16,64,1,4,128]{4,1,3,2,0:T(8,128)S(1)} async-done(((f32[16,64,1,4,128]{4,1,3,2,0:T(8,128)}), f32[16,64,1,4,128]{4,1,3,2,0:T(8,128)S(1)}, u32[]{:S(2)}, u32[]{:S(2)}) %all-to-all-start.1) | async-done | bytes 2097184 | tf_op jit(solution)/shard_map/all_to_all | solution.py:118
  92.4 0.7 bitcast_reduce_fusion
  93.3 2.9 fusion.26
  96.3 1.3 copy-done.2
  98.1 0.6 reduce-window.19
  99.4 60.5 %all-reduce.2.cloned.1.call-done = f32[128,4096]{1,0:T(8,128)} async-done(((f32[128,4096]{1,0:T(8,128)}), f32[128,4096]{1,0:T(8,128)}) %all-reduce.2.cloned.1.call-update) | async-done | bytes 2097168 | tf_op jit(solution)/shard_map/psum | solution.py:170
  159.9 2.0 multiply_reduce_fusion
  162.1 1.1 convolution_convert_fusion.1
  163.2 0.8 broadcast_in_dim.146
  164.0 79.0 %all_to_all.30 = bf16[16,48,4096]{2,1,0:T(8,128)(2,1)S(1)} all-to-all(bf16[16,48,4096]{2,1,0:T(8,128)(2,1)S(1)} %bitcast.149), channel_id=1, replica_groups=mesh['dp'=16,'mp'=8] {'dp'}, dimensions={0} | all-to-all | bytes 12582912 | tf_op jit(solution)/shard_map/all_to_all | solution.py:190
  243.0 7.5 %fusion.1 = f32[16,48,768]{2,1,0:T(8,128)S(1)} fusion(bf16[16,48,4096]{2,1,0:T(8,128)(2,1)S(1)} %all_to_all.30, bf16[4096,768]{1,0:T(8,128)(2,1)} %param.29), kind=kOutput, calls=%fused_computation.4 | convolution fusion | flops 4831838208 | bytes 14942208 | tf_op jit(solution)/shard_map/scd,df->scf/dot_general | solution.py:192
  250.5 5.3 %multiply_convert_fusion = bf16[16,48,768]{2,1,0:T(8,128)(2,1)S(1)} fusion(f32[16,48,768]{2,1,0:T(8,128)S(1)} %fusion.1, bf16[16,48,4096]{2,1,0:T(8,128)(2,1)S(1)} %all_to_all.30, bf16[4096,768]{1,0:T(8,128)(2,1)S(1)} %bitcast.157), kind=kOutput, calls=%fused_computation.9 | convolution fusion | flops 4835377152 | bytes 16121856 | tf_op jit(solution)/shard_map/scd,df->scf/dot_general | solution.py:191
  255.9 6.9 %convolution_convert_fusion = bf16[16,48,4096]{2,1,0:T(8,128)(2,1)} fusion(bf16[16,48,768]{2,1,0:T(8,128)(2,1)S(1)} %multiply_convert_fusion, bf16[768,4096]{1,0:T(8,128)(2,1)S(1)} %bitcast.159), kind=kOutput, calls=%fused_computation.2 | convolution fusion | flops 4834983936 | bytes 13762560 | tf_op jit(solution)/shard_map/scf,fd->scd/dot_general | solution.py:194
  262.8 41.5 %reduce-scatter.2.cloned.1.call-done = bf16[16,48,512]{2,1,0:T(8,128)(2,1)} async-done(((bf16[16,48,4096]{2,1,0:T(8,128)(2,1)}), bf16[16,48,512]{2,1,0:T(8,128)(2,1)}) %reduce-scatter.2.cloned.1.call-update) | async-done | bytes 786448 | tf_op jit(solution)/shard_map/reduce_scatter | solution.py:195
  304.3 2.5 convert_element_type.63
  306.8 7.0 %all-to-all-start.5 = ((f32[16,48,512]{2,1,0:T(8,128)}), f32[16,48,512]{2,1,0:T(8,128)}, u32[]{:S(2)}, u32[]{:S(2)}) async-start(f32[16,48,512]{2,1,0:T(8,128)} %convert_element_type.63), calls=%async_computation.6 | async-start | bytes 3145728 | tf_op jit(solution)/shard_map/all_to_all | solution.py:198
  314.0 23.3 %all-to-all-done.5 = f32[16,48,512]{2,1,0:T(8,128)} async-done(((f32[16,48,512]{2,1,0:T(8,128)}), f32[16,48,512]{2,1,0:T(8,128)}, u32[]{:S(2)}, u32[]{:S(2)}) %all-to-all-start.5) | async-done | bytes 1572896 | tf_op jit(solution)/shard_map/all_to_all | solution.py:198
  337.3 1.6 bitcast_reduce_fusion.1
  339.0 0.7 multiply_reduce_fusion.1
  339.7 17.0 %psum.15 = f32[128]{0:T(128)S(1)} all-reduce(f32[128]{0:T(128)S(1)} %get-tuple-element.20), channel_id=1, replica_groups=mesh['dp'=16,'mp'=8] {'mp'}, use_global_device_ids=true, to_apply=%region_24.25 | all-reduce | flops 128 | bytes 1024 | tf_op jit(solution)/shard_map/psum | solution.py:206
  356.7 0.8 multiply_convert_fusion.3
  (95 shorter events, 4.2 us)
Async XLA Ops:
  6.5 36.1 %copy-start = (bf16[128,16,128]{2,1,0:T(8,128)(2,1)S(1)}, bf16[128,16,128]{2,1,0:T(8,128)(2,1)}, u32[]{:S(2)}) copy-start(bf16[128,16,128]{2,1,0:T(8,128)(2,1)} %param.21) | copy-start | bytes 1572868
  6.5 10.3 %copy-start.6 = (s32[1024]{0:T(1024)S(1)}, s32[1024]{0:T(1024)}, u32[]{:S(2)}) copy-start(s32[1024]{0:T(1024)} %param.22) | copy-start | bytes 12292
  6.5 10.9 %copy-start.10 = (s32[2048]{0:T(1024)S(1)}, s32[2048]{0:T(1024)}, u32[]{:S(2)}) copy-start(s32[2048]{0:T(1024)} %param.23) | copy-start | bytes 24580
  8.6 26.9 %copy-start.4 = (bf16[128,16,128]{2,1,0:T(8,128)(2,1)S(1)}, bf16[128,16,128]{2,1,0:T(8,128)(2,1)}, u32[]{:S(2)}) copy-start(bf16[128,16,128]{2,1,0:T(8,128)(2,1)} %param.20) | copy-start | bytes 1572868
  8.6 25.9 %all-to-all-start = ((bf16[16,64,512]{2,1,0:T(8,128)(2,1)}), bf16[16,64,512]{2,1,0:T(8,128)(2,1)S(1)}, u32[]{:S(2)}, u32[]{:S(2)}) async-start(bf16[16,64,512]{2,1,0:T(8,128)(2,1)} %stack.2), calls=%async_computation | async-start | bytes 2097152 | tf_op jit(solution)/shard_map/all_to_all | solution.py:96
  39.1 11.0 %all-to-all-start.3 = ((f32[16,1,256]{2,1,0:T(1,128)}), f32[16,1,256]{2,1,0:T(1,128)S(1)}, u32[]{:S(2)}, u32[]{:S(2)}) async-start(f32[16,1,256]{2,1,0:T(1,128)} %reshape.466), calls=%async_computation.3 | async-start | bytes 32768 | tf_op jit(solution)/shard_map/all_to_all | solution.py:117
  50.2 11.0 %all-to-all-start.2 = ((f32[16,1,256]{2,1,0:T(1,128)}), f32[16,1,256]{2,1,0:T(1,128)S(1)}, u32[]{:S(2)}, u32[]{:S(2)}) async-start(f32[16,1,256]{2,1,0:T(1,128)} %reshape.464), calls=%async_computation.2 | async-start | bytes 32768 | tf_op jit(solution)/shard_map/all_to_all | solution.py:116
  56.1 8.9 %copy-start.7 = (bf16[128,128]{1,0:T(8,128)(2,1)S(1)}, bf16[128,128]{1,0:T(8,128)(2,1)}, u32[]{:S(2)}) copy-start(bf16[128,128]{1,0:T(8,128)(2,1)} %param.18) | copy-start | bytes 98308
  56.1 9.5 %copy-start.9 = (bf16[128,128]{1,0:T(8,128)(2,1)S(1)}, bf16[128,128]{1,0:T(8,128)(2,1)}, u32[]{:S(2)}) copy-start(bf16[128,128]{1,0:T(8,128)(2,1)} %param.19) | copy-start | bytes 98308
  61.2 31.2 %all-to-all-start.1 = ((f32[16,64,1,4,128]{4,1,3,2,0:T(8,128)}), f32[16,64,1,4,128]{4,1,3,2,0:T(8,128)S(1)}, u32[]{:S(2)}, u32[]{:S(2)}) async-start(f32[16,64,1,4,128]{4,1,3,2,0:T(8,128)} %convolution_bitcast_fusion), calls=%async_computation.1 | async-start | bytes 4194304 | tf_op jit(solution)/shard_map/all_to_all | solution.py:118
  64.9 95.0 %all-reduce.2.cloned.1.call-start = ((), (), s32[]{:S(2)}) async-start(), calls=%async_computation.7 | async-start | bytes 4194304 | tf_op jit(solution)/shard_map/psum | solution.py:170
  93.3 3.0 copy-start.5
  96.2 1.4 copy-start.11
  96.3 1.3 copy-start.2
  96.3 65.6 %copy-start.8 = (f32[4096]{0:T(1024)S(1)}, f32[4096]{0:T(1024)}, u32[]{:S(2)}) copy-start(f32[4096]{0:T(1024)} %param.25) | copy-start | bytes 49156
  97.6 206.7 %reduce-scatter.2.cloned.1.call-start = ((), (), s32[]{:S(2)}) async-start(), calls=%async_computation.8 | async-start | bytes 7077888 | tf_op jit(solution)/shard_map/reduce_scatter | solution.py:195
  159.9 2.2 copy-start.3
  164.0 86.5 %slice-start = ((s8[6291456]{0:T(1024)(128)(4,1)}), s8[4194304]{0:T(1024)(128)(4,1)S(1)}, s32[]{:S(2)}) async-start(s8[6291456]{0:T(1024)(128)(4,1)} %bitcast.156), calls=%async_computation.9 | async-start | bytes 8388608
  243.0 7.5 %slice-start.1 = ((s8[6291456]{0:T(1024)(128)(4,1)}), s8[2097152]{0:T(1024)(128)(4,1)S(1)}, s32[]{:S(2)}) async-start(s8[6291456]{0:T(1024)(128)(4,1)} %bitcast.156), calls=%async_computation.10 | async-start | bytes 4194304
  243.0 12.8 %slice-start.2 = ((s8[6291456]{0:T(1024)(128)(4,1)}), s8[4194304]{0:T(1024)(128)(4,1)S(1)}, s32[]{:S(2)}) async-start(s8[6291456]{0:T(1024)(128)(4,1)} %bitcast.158), calls=%async_computation.11 | async-start | bytes 8388608
  250.5 5.3 %slice-start.3 = ((s8[6291456]{0:T(1024)(128)(4,1)}), s8[2097152]{0:T(1024)(128)(4,1)S(1)}, s32[]{:S(2)}) async-start(s8[6291456]{0:T(1024)(128)(4,1)} %bitcast.158), calls=%async_computation.12 | async-start | bytes 4194304
  262.8 51.1 %copy-start.13 = (f32[128,2]{0,1:T(2,128)S(1)}, f32[128,2]{0,1:T(2,128)}, u32[]{:S(2)}) copy-start(f32[128,2]{0,1:T(2,128)} %param.27) | copy-start | bytes 3076
  306.8 30.5 %all-to-all-start.5 = ((f32[16,48,512]{2,1,0:T(8,128)}), f32[16,48,512]{2,1,0:T(8,128)}, u32[]{:S(2)}, u32[]{:S(2)}) async-start(f32[16,48,512]{2,1,0:T(8,128)} %convert_element_type.63), calls=%async_computation.6 | async-start | bytes 3145728 | tf_op jit(solution)/shard_map/all_to_all | solution.py:198
  313.9 42.8 %copy-start.12 = (f32[512]{0:T(512)S(1)}, f32[512]{0:T(512)}, u32[]{:S(2)}) copy-start(f32[512]{0:T(512)} %param.31) | copy-start | bytes 6148
  313.9 43.6 %copy-start.1 = (bf16[128,16,128]{2,1,0:T(8,128)(2,1)S(1)}, bf16[128,16,128]{2,1,0:T(8,128)(2,1)}, u32[]{:S(2)}) copy-start(bf16[128,16,128]{2,1,0:T(8,128)(2,1)} %param.21) | copy-start | bytes 1572868
Sparse Core Ops, SparseCore 0:
  97.7 62.1 all-reduce.1
  262.9 41.3 reduce-scatter.1
